TPU v7x, 32 devices: a whole 2x2x4 slice. The times are simulated.
32 devices in a mesh: ctx: 2 (over core), section: 4 (over y, x), dp: 4 (over z).
Axes of the slice: x: 2, y: 2, z: 4, core: 2. Of those that a mesh axis runs over, the one named last changes fastest.
Arguments:
- conv_input: bfloat16 [4, 4, 256, 5120], P('section', 'dp', 'ctx'), may hold values from -6 to 6
- gate_input: bfloat16 [4, 4, 256, 1024], P('section', 'dp', 'ctx'), may hold values from -6 to 6
- step_input: bfloat16 [4, 4, 256, 16], P('section', 'dp', 'ctx'), may hold values from -7 to 3
- cotangent: bfloat16 [4, 4, 256, 1024], P('section', 'dp', 'ctx'), may hold values from -6 to 6
- conv_weight: float32 [4, 4, 5120], P('section'), may hold values from -3 to 3
- conv_bias: float32 [4, 5120], P('section'), may hold values from -0.5 to 0.5
- step_bias: float32 [4, 16], P('section'), may hold values from -0.5 to 0.5
- decay_log: float32 [4, 16], P('section'), may hold values from -6 to 0.3
- skip_gain: float32 [4, 16], P('section'), may hold values from 0.5 to 1.5
- norm_gain: float32 [4, 1024], P('section'), may hold values from 0.5 to 1.5
Outputs:
- next_input: bfloat16 [4, 4, 256, 1024], P('section', 'dp', 'ctx')
- grad_conv_input: bfloat16 [4, 4, 256, 5120], P('section', 'dp', 'ctx')
- grad_gate_input: bfloat16 [4, 4, 256, 1024], P('section', 'dp', 'ctx')
- grad_step_input: bfloat16 [4, 4, 256, 16], P('section', 'dp', 'ctx')
- kernel_filter_derivative: float32 [4, 4, 5120], P('section')
- grad_conv_bias: float32 [4, 5120], P('section')
- grad_step_bias: float32 [4, 16], P('section')
- grad_decay_log: float32 [4, 16], P('section')
- grad_skip_gain: float32 [4, 16], P('section')
- grad_norm_gain: float32 [4, 1024], P('section')
All inputs are finite; a program needn't handle non-finite values.
Results may differ from a plain program's by a relative error of at most 0.0026.
Values may be sent and summed in bfloat16 or wider, within the bound.
A program may use at most 128 MiB of HBM per device.

v0:
```python
import functools
import jax
import jax.numpy as jnp
from jax import lax
from jax.experimental import pallas as pl
from jax.experimental.pallas import tpu as pltpu
from jax.sharding import PartitionSpec as P

HEADS = 16
HEAD_DIM = 64
STATE = 256
GROUPS = 8
CONV = 4


HIGH_BOUND = lax.Precision.HIGHEST


def shifted(block, axis, distance):
    devices = range(lax.axis_size(axis))
    route = [(i - distance, i) for i in devices if i - distance in devices]
    return lax.ppermute(block, axis, route)


def prefix(part, axis, combine, identity):
    count = lax.axis_size(axis)
    place = lax.axis_index(axis)
    ahead = count - 1 - place
    gathered = jax.tree.map(lambda a: lax.all_gather(a, axis), part)
    state = jax.tree.map(lambda a, e: jnp.zeros_like(a) + jnp.asarray(e, a.dtype), part, identity)

    def one(turn, state):
        source = count - 1 - turn
        return combine(
            state, jax.tree.map(lambda a: lax.dynamic_index_in_dim(a, source, 0, False), gathered)
        )

    return lax.fori_loop(0, ahead, one, state)


def conv_mix(extended, taps, initial_offset):
    rows = extended.shape[0] - (CONV - 1)
    total = initial_offset[None, :]
    for tap in range(CONV):
        total = total + taps[tap][None, :] * extended[tap : tap + rows]
    return jax.nn.silu(total)


def split_mix(mixed, steps, step_shift, damping_exponents):
    rows = mixed.shape[0]
    inner = HEADS * HEAD_DIM
    payload_lines = mixed[:, :inner].reshape(rows, GROUPS, HEADS // GROUPS, HEAD_DIM)
    in_maps = mixed[:, inner : inner + GROUPS * STATE].reshape(rows, GROUPS, STATE)
    out_maps = mixed[:, inner + GROUPS * STATE :].reshape(rows, GROUPS, STATE)
    delta = jax.nn.softplus(steps + step_shift[None, :])
    cumulative = jnp.cumsum(delta * (-jnp.exp(damping_exponents))[None, :], axis=0)
    return (payload_lines, in_maps, out_maps, delta, cumulative)


def fragment_condition(extended, steps, taps, initial_offset, step_shift, damping_exponents):
    payload_lines, in_maps, out_maps, delta, cumulative = split_mix(
        conv_mix(extended, taps, initial_offset), steps, step_shift, damping_exponents
    )
    rows = payload_lines.shape[0]
    total = cumulative[-1]
    weight = (jnp.exp(total[None, :] - cumulative) * delta).reshape(rows, GROUPS, HEADS // GROUPS)
    state = jnp.einsum(
        "tgrp,tgn->grpn", payload_lines * weight[..., None], in_maps, precision=HIGH_BOUND
    )
    return (state.reshape(HEADS, HEAD_DIM, STATE), total)


def shard_layer(
    extended,
    gates,
    steps,
    taps,
    initial_offset,
    step_shift,
    damping_exponents,
    skip_values,
    gain_values,
    carried,
):
    payload_lines, in_maps, out_maps, delta, cumulative = split_mix(
        conv_mix(extended, taps, initial_offset), steps, step_shift, damping_exponents
    )
    rows = payload_lines.shape[0]
    reps = HEADS // GROUPS
    lower = (jnp.arange(rows)[:, None] >= jnp.arange(rows)[None, :])[None]
    seg = cumulative.T[:, :, None] - cumulative.T[:, None, :]
    weight = jnp.exp(jnp.where(lower, seg, -jnp.inf)).reshape(GROUPS, reps, rows, rows)
    intersection_maps = jnp.einsum("tgn,sgn->gts", out_maps, in_maps, precision=HIGH_BOUND)
    score_matrix = weight * intersection_maps[:, None]
    scaled_values = payload_lines * delta.reshape(rows, GROUPS, reps)[..., None]
    final_output = jnp.einsum("jzlh,hjzc->ljzc", score_matrix, scaled_values, precision=HIGH_BOUND)
    incoming = jnp.einsum(
        "tgn,grpn->tgrp",
        out_maps,
        carried.reshape(GROUPS, reps, HEAD_DIM, STATE),
        precision=HIGH_BOUND,
    )
    final_output = (
        final_output + incoming * jnp.exp(cumulative).reshape(rows, GROUPS, reps)[..., None]
    )
    final_output = (
        final_output + skip_values.reshape(GROUPS, reps)[None, :, :, None] * payload_lines
    )
    gated = final_output.reshape(rows, GROUPS, -1) * jax.nn.silu(gates).reshape(rows, GROUPS, -1)
    normed = gated * lax.rsqrt(jnp.mean(gated * gated, axis=-1, keepdims=True) + 1e-05)
    return normed.reshape(rows, -1) * gain_values[None, :]


def combine(earlier, later):
    return (earlier[0] * later[0], later[0][:, None] * earlier[1] + later[1])


def shards(
    conv_input,
    gate_input,
    step_input,
    cotangent,
    conv_weight,
    conv_bias,
    step_bias,
    decay_log,
    skip_gain,
    norm_gain,
):
    local_rows = conv_input[0, 0]
    count = local_rows.shape[0]
    taps, initial_offset = (conv_weight[0], conv_bias[0])
    step_shift, damping_exponents = (step_bias[0], decay_log[0])
    skip_values, gain_values = (skip_gain[0], norm_gain[0])
    previous = shifted(local_rows[count - (CONV - 1) :], "ctx", 1)
    extended = jnp.concatenate([previous, local_rows], 0).astype(jnp.float32)
    gates = gate_input[0, 0].astype(jnp.float32)
    steps = step_input[0, 0].astype(jnp.float32)
    (state, total), state_pull = jax.vjp(
        fragment_condition, extended, steps, taps, initial_offset, step_shift, damping_exponents
    )
    decay = jnp.exp(total)
    flat_state = state.reshape(HEADS, HEAD_DIM * STATE)
    unity = (jnp.ones((HEADS,), jnp.float32), jnp.zeros((HEADS, HEAD_DIM * STATE), jnp.float32))

    def advance(index, current):
        return shifted(decay[:, None] * current + flat_state, "ctx", 1)

    incoming = lax.fori_loop(
        0, lax.axis_size("ctx") - 1, advance, jnp.zeros((HEADS, HEAD_DIM * STATE), jnp.float32)
    )
    carried = incoming.reshape(HEADS, HEAD_DIM, STATE)
    final_output, layer_pull = jax.vjp(
        shard_layer,
        extended,
        gates,
        steps,
        taps,
        initial_offset,
        step_shift,
        damping_exponents,
        skip_values,
        gain_values,
        carried,
    )
    forward = shifted(final_output.astype(jnp.bfloat16)[None, None], "section", 1)
    grads = layer_pull(cotangent[0, 0].astype(jnp.float32))
    carry_grad = grads[9].reshape(HEADS, HEAD_DIM * STATE)
    outgoing = prefix((decay, carry_grad), "ctx", combine, unity)[1]
    outgoing_grad = outgoing.reshape(HEADS, HEAD_DIM, STATE)
    total_grad = jnp.sum(outgoing_grad * carried, axis=(1, 2)) * decay
    extra = state_pull((outgoing_grad, total_grad))
    ext_grad = grads[0] + extra[0]
    step_grad = grads[2] + extra[1]
    param_terms = (
        grads[3] + extra[2],
        grads[4] + extra[3],
        grads[5] + extra[4],
        grads[6] + extra[5],
        grads[7],
        grads[8],
    )
    returned = shifted(ext_grad[: CONV - 1], "ctx", -1)
    own_grad = ext_grad[CONV - 1 :]
    row_grad = jnp.concatenate(
        [own_grad[: count - (CONV - 1)], own_grad[count - (CONV - 1) :] + returned], 0
    )
    backward = shifted(
        (
            row_grad.astype(jnp.bfloat16)[None, None],
            grads[1].astype(jnp.bfloat16)[None, None],
            step_grad.astype(jnp.bfloat16)[None, None],
        ),
        "section",
        -1,
    )
    summed = lax.psum(
        (
            param_terms[0],
            param_terms[1],
            param_terms[2],
            param_terms[3],
            param_terms[4],
            param_terms[5],
        ),
        ("ctx", "dp"),
    )
    return (
        forward,
        backward[0],
        backward[1],
        backward[2],
        summed[0][None],
        summed[1][None],
        summed[2][None],
        summed[3][None],
        summed[4][None],
        summed[5][None],
    )


MESH = pl.DeviceIdType.MESH
F32 = jnp.float32
BF16 = jnp.bfloat16
INNER = HEADS * HEAD_DIM
REPS = HEADS // GROUPS
WIDE = REPS * HEAD_DIM
MIX = WIDE + 2 * STATE
HALF = GROUPS // 2
NN = ((1,), (0,))
NT = ((1,), (1,))
TN = ((0,), (0,))


def split(a):
    high = a.astype(BF16)
    return high, (a - high.astype(F32)).astype(BF16)


def dot(a, b, dims):
    return lax.dot_general(a, b, (dims, ((), ())), preferred_element_type=F32)


def dot3(a, b, dims):
    return dot(a[0], b[0], dims) + (dot(a[0], b[1], dims) + dot(a[1], b[0], dims))


def group_columns(g):
    return (
        pl.multiple_of(g * WIDE, 128),
        pl.multiple_of(INNER + g * STATE, 128),
        pl.multiple_of(INNER + (GROUPS + g) * STATE, 128),
    )


def pair_kernel(
    conv_in, gate_in, step_in, cot_in, w_ref, b_ref, sb_ref, dl_ref, sk_ref, ng_ref,
    nxt, gconv, ggate, gstep, gtap, gcb, gsb, gdl, gsk, gng,
    uin, steps, upad, zpad, mix, dsl, dtc, sigc, ratec, cumc, cumr, ddt, drate, small,
    stage_c, stage_o, stage_s, step_parts, partial, final, zeros,
    own_sem, xs_sem, xr_sem, st_sem, conv_sem, gate_sem, next_sem, dstep_sem,
    ps_sem, pr_sem, fin_sem, zero_sem,
):
    core = lax.axis_index("ctx")
    sec = lax.axis_index("section")
    dp = lax.axis_index("dp")
    nsec = lax.axis_size("section")
    ndp = lax.axis_size("dp")
    tok = conv_in.shape[2]
    seq = 2 * tok
    other = 1 - core

    def place(c, s, d):
        return {"ctx": c, "section": s, "dp": d}

    def remote(src, dst, send, recv, c, s, d):
        return pltpu.make_async_remote_copy(
            src_ref=src, dst_ref=dst, send_sem=send, recv_sem=recv,
            device_id=place(c, s, d), device_id_type=MESH,
        )

    after = lax.rem(sec + 1, nsec)
    before = lax.rem(sec + nsec - 1, nsec)
    barrier = pltpu.get_barrier_semaphore()

    def greet(c, s, d):
        pl.semaphore_signal(barrier, inc=1, device_id=place(c, s, d), device_id_type=MESH)

    greet(other, sec, dp)
    for c in range(2):
        greet(c, after, dp)
        greet(c, before, dp)
    for k in range(1, ndp):
        greet(core, sec, lax.rem(dp + k, ndp))

    def pieces(g):
        xc, bc, cc = group_columns(g)
        return (
            (conv_in.at[0, 0, :, pl.ds(xc, WIDE)], 0, WIDE),
            (conv_in.at[0, 0, :, pl.ds(bc, STATE)], WIDE, STATE),
            (conv_in.at[0, 0, :, pl.ds(cc, STATE)], WIDE + STATE, STATE),
            (gate_in.at[0, 0, :, pl.ds(xc, WIDE)], MIX, WIDE),
            (cot_in.at[0, 0, :, pl.ds(xc, WIDE)], MIX + WIDE, WIDE),
        )

    mine = pl.ds(pl.multiple_of(core * tok, tok), tok)
    theirs = pl.ds(pl.multiple_of(other * tok, tok), tok)
    own_step = pltpu.make_async_copy(step_in.at[0, 0], steps.at[core], st_sem.at[0])
    own_step.start()

    def fetch(j, _):
        for src, off, width in pieces(core * HALF + j):
            pltpu.make_async_copy(
                src, uin.at[j, mine, pl.ds(off, width)], own_sem.at[j]
            ).start()
        return 0

    lax.fori_loop(0, HALF, fetch, 0)
    zeros[...] = jnp.zeros_like(zeros)
    partial[dp] = jnp.zeros(partial.shape[1:], F32)
    upad[0:8, :] = jnp.zeros((8, MIX), F32)
    zpad[seq : seq + 8, :] = jnp.zeros((8, MIX), F32)
    for ref in (dtc, sigc, ratec, ddt, drate, small):
        ref[...] = jnp.zeros_like(ref)
    pl.semaphore_wait(barrier, 1 + 4 + (ndp - 1))
    step_copy = remote(
        step_in.at[0, 0], steps.at[core], st_sem.at[1], st_sem.at[2], other, sec, dp
    )
    step_copy.start()

    def exchange(j, _):
        for src, off, width in pieces(other * HALF + j):
            remote(
                src, uin.at[j, mine, pl.ds(off, width)], xs_sem.at[j], xr_sem.at[j], other, sec, dp
            ).start()
        return 0

    lax.fori_loop(0, HALF, exchange, 0)

    @pl.when(sec == 0)
    def _():
        pltpu.make_async_copy(zeros, nxt.at[0, 0], zero_sem.at[0]).start()

    @pl.when(sec == nsec - 1)
    def _():
        for part in range(5):
            pltpu.make_async_copy(
                zeros, gconv.at[0, 0, :, pl.ds(part * INNER, INNER)], zero_sem.at[1]
            ).start()
        pltpu.make_async_copy(zeros, ggate.at[0, 0], zero_sem.at[2]).start()

    own_step.wait()
    step_copy.wait()
    raw = steps[...].astype(F32).reshape(seq, HEADS) + sb_ref[...]
    delta = jnp.maximum(raw, 0.0) + jnp.log1p(jnp.exp(-jnp.abs(raw)))
    dtc[:, 0:HEADS] = delta
    sigc[:, 0:HEADS] = jax.nn.sigmoid(raw)
    ratec[:, 0:HEADS] = delta * (-jnp.exp(dl_ref[...]))
    rows2 = lax.broadcasted_iota(jnp.int32, (seq, seq), 0)
    cols2 = lax.broadcasted_iota(jnp.int32, (seq, seq), 1)
    ones_low = jnp.where(rows2 >= cols2, 1.0, 0.0).astype(BF16)
    rate = ratec[...]
    r_hi, r_rest = rate.astype(BF16), rate - rate.astype(BF16).astype(F32)
    r_mid, r_lo = split(r_rest)
    cumulative = dot(ones_low, r_hi, NN) + (dot(ones_low, r_mid, NN) + dot(ones_low, r_lo, NN))
    cumc[...] = cumulative
    cumr[...] = cumulative.T

    def group(j, _):
        g = core * HALF + j
        cols = group_columns(g)
        pltpu.make_async_copy(uin.at[j, mine], uin.at[j, mine], own_sem.at[j]).wait()
        remote(uin.at[j, mine], uin.at[j, theirs], xs_sem.at[j], xr_sem.at[j], other, sec, dp).wait()
        blocks = [(0, cols[0])]
        for base, col in ((WIDE, cols[1]), (WIDE + STATE, cols[2])):
            for part in range(STATE // 128):
                blocks.append((base + part * 128, pl.multiple_of(col + part * 128, 128)))

        for off, col in blocks:
            here = slice(off, off + 128)
            upad[8 : 8 + seq, here] = uin[j, :, here].astype(F32)
            z = b_ref[:, pl.ds(col, 128)]
            for k in range(CONV):
                z = z + w_ref[0, pl.ds(k, 1), pl.ds(col, 128)] * upad[5 + k : 5 + k + seq, here]
            s = jax.nn.sigmoid(z)
            mix[:, here] = z * s
            dsl[:, here] = s * (1.0 + z * (1.0 - s))

        lane = lax.broadcasted_iota(jnp.int32, (seq, 128), 1)
        lane1 = lax.broadcasted_iota(jnp.int32, (1, 128), 1)
        lane16 = lax.broadcasted_iota(jnp.int32, (1, HEADS), 1)
        row = lax.broadcasted_iota(jnp.int32, (seq, seq), 0)
        column = lax.broadcasted_iota(jnp.int32, (seq, seq), 1)
        first = lane < HEAD_DIM

        def pick(ref, h):
            return jnp.sum(jnp.where(lane == h, ref[...], 0.0), axis=1, keepdims=True)

        def pick1(ref, h):
            return jnp.sum(jnp.where(lane16 == h, ref[...], 0.0), axis=1, keepdims=True)

        x = mix[:, 0:WIDE]
        bmap = split(mix[:, WIDE : WIDE + STATE])
        cmap = split(mix[:, WIDE + STATE : MIX])
        h0 = g * REPS
        dt2 = jnp.where(first, pick(dtc, h0), pick(dtc, h0 + 1))
        skip2 = jnp.where(first[0:1], pick1(sk_ref, h0), pick1(sk_ref, h0 + 1))
        xs = x * dt2
        xs_p = split(xs)
        scores = dot3(cmap, bmap, NT)
        decay, mixed, ys = [], [], []
        for r in range(REPS):
            seg = pick(cumc, h0 + r) - cumr[pl.ds(h0 + r, 1), :]
            w = jnp.exp(jnp.where(row >= column, seg, -jnp.inf))
            a = scores * w
            a_p = split(a)
            decay.append(w)
            mixed.append((a, a_p))
            ys.append(dot3(a_p, xs_p, NN))
        y = jnp.where(first, ys[0], ys[1]) + skip2 * x
        gate = uin[j, :, MIX : MIX + WIDE].astype(F32)
        cot = uin[j, :, MIX + WIDE : MIX + 2 * WIDE].astype(F32)
        gain = ng_ref[:, pl.ds(cols[0], WIDE)]
        s = jax.nn.sigmoid(gate)
        act = gate * s
        gated = y * act
        scale = lax.rsqrt(jnp.mean(gated * gated, axis=1, keepdims=True) + 1e-05)
        normed = gated * scale
        stage_o[j, :, 0:WIDE] = (normed * gain).astype(BF16)
        dn = cot * gain
        dgated = scale * (dn - normed * jnp.mean(dn * normed, axis=1, keepdims=True))
        dy = dgated * act
        stage_o[j, :, WIDE : 2 * WIDE] = (dgated * y * (s * (1.0 + gate * (1.0 - s)))).astype(BF16)

        @pl.when(sec < nsec - 1)
        def _():
            for t in range(2):
                remote(
                    stage_o.at[j, pl.ds(t * tok, tok), pl.ds(0, WIDE)],
                    nxt.at[0, 0, :, pl.ds(cols[0], WIDE)],
                    next_sem.at[0], next_sem.at[1], t, sec + 1, dp,
                ).start()

        @pl.when(sec > 0)
        def _():
            for t in range(2):
                remote(
                    stage_o.at[j, pl.ds(t * tok, tok), pl.ds(WIDE, WIDE)],
                    ggate.at[0, 0, :, pl.ds(cols[0], WIDE)],
                    gate_sem.at[0], gate_sem.at[1], t, sec - 1, dp,
                ).start()

        partial[dp, j, 5:6, 0:WIDE] = jnp.sum(cot * normed, axis=0, keepdims=True)
        dyx = jnp.sum(dy * x, axis=0, keepdims=True)
        dscore = jnp.zeros((seq, seq), F32)
        dxs = []
        upper = jnp.where(row <= column, 1.0, 0.0).astype(BF16)
        dy_p = split(dy)
        for r in range(REPS):
            own = first if r == 0 else jnp.logical_not(first)
            dyr_p = split(jnp.where(own, dy, 0.0))
            da = dot3(dyr_p, xs_p, NT)
            dscore = dscore + da * decay[r]
            p = split(da * mixed[r][0])
            later = dot(upper, p[0], NN) + dot(upper, p[1], NN)
            dr = jnp.sum(jnp.where(row > column, later, 0.0), axis=1, keepdims=True)
            drate[...] += jnp.where(lane == h0 + r, dr, 0.0)
            dxs.append(dot3(mixed[r][1], dy_p, TN))
            total = jnp.sum(jnp.where(own[0:1], dyx, 0.0), axis=1, keepdims=True)
            small[2:3, :] += jnp.where(lane1 == h0 + r, total, 0.0)
        dxs = jnp.where(first, dxs[0], dxs[1])
        dxx = dxs * x
        ddt[...] += jnp.where(
            lane == h0, jnp.sum(jnp.where(first, dxx, 0.0), axis=1, keepdims=True), 0.0
        ) + jnp.where(
            lane == h0 + 1, jnp.sum(jnp.where(first, 0.0, dxx), axis=1, keepdims=True), 0.0
        )
        ds_p = split(dscore)
        zpad[0:seq, 0:WIDE] = (skip2 * dy + dxs * dt2) * dsl[:, 0:WIDE]
        zpad[0:seq, WIDE : WIDE + STATE] = dot3(ds_p, cmap, TN) * dsl[:, WIDE : WIDE + STATE]
        zpad[0:seq, WIDE + STATE : MIX] = dot3(ds_p, bmap, NN) * dsl[:, WIDE + STATE : MIX]
        for off, col in blocks:
            here = slice(off, off + 128)
            dz = zpad[0:seq, here]
            du = jnp.zeros((seq, 128), F32)
            for k in range(CONV):
                du = du + w_ref[0, pl.ds(k, 1), pl.ds(col, 128)] * zpad[3 - k : 3 - k + seq, here]
                partial[dp, j, pl.ds(k, 1), here] = jnp.sum(
                    dz * upad[5 + k : 5 + k + seq, here], axis=0, keepdims=True
                )
            partial[dp, j, pl.ds(4, 1), here] = jnp.sum(dz, axis=0, keepdims=True)
            stage_c[j, :, here] = du.astype(BF16)

        @pl.when(sec > 0)
        def _():
            for t in range(2):
                for off, width, col in (
                    (0, WIDE, cols[0]), (WIDE, STATE, cols[1]), (WIDE + STATE, STATE, cols[2])
                ):
                    remote(
                        stage_c.at[j, pl.ds(t * tok, tok), pl.ds(off, width)],
                        gconv.at[0, 0, :, pl.ds(col, width)],
                        conv_sem.at[0], conv_sem.at[1], t, sec - 1, dp,
                    ).start()

        for k in range(1, ndp):
            to = lax.rem(dp + k, ndp)
            remote(
                partial.at[dp, j], partial.at[dp, j], ps_sem.at[to], pr_sem.at[dp], core, sec, to
            ).start()
        return 0

    lax.fori_loop(0, HALF, group, 0)

    damp = jnp.exp(dl_ref[...])
    dr16 = drate[:, 0:HEADS]
    dstep = (ddt[:, 0:HEADS] - dr16 * damp) * sigc[:, 0:HEADS]
    small[0:1, 0:HEADS] = jnp.sum(dstep, axis=0, keepdims=True)
    small[1:2, 0:HEADS] = jnp.sum(dr16 * ratec[:, 0:HEADS], axis=0, keepdims=True)
    stage_s[...] = jnp.zeros_like(stage_s)
    stage_s[:, 0:HEADS] = dstep.astype(BF16)

    @pl.when(sec > 0)
    def _():
        for t in range(2):
            remote(
                stage_s.at[pl.ds(t * tok, tok)], step_parts.at[core],
                dstep_sem.at[2], dstep_sem.at[core], t, sec - 1, dp,
            ).start()

    partial[dp, HALF, :, 0:128] = small[...]
    for k in range(1, ndp):
        to = lax.rem(dp + k, ndp)
        remote(
            partial.at[dp, HALF], partial.at[dp, HALF], ps_sem.at[to], pr_sem.at[dp], core, sec, to
        ).start()
    for k in range(1, ndp):
        to = lax.rem(dp + k, ndp)
        remote(partial.at[dp], partial.at[to], ps_sem.at[to], pr_sem.at[to], core, sec, to).wait()
    total = partial[0]
    for k in range(1, ndp):
        total = total + partial[k]
    final[core] = total
    halves = remote(final.at[core], final.at[core], fin_sem.at[0], fin_sem.at[1], other, sec, dp)
    halves.start()
    remote(final.at[core], final.at[other], fin_sem.at[0], fin_sem.at[1], other, sec, dp).wait()
    for g in range(GROUPS):
        c, j = g // HALF, g % HALF
        gng[0:1, g * WIDE : (g + 1) * WIDE] = final[c, j, 5:6, 0:WIDE]
        for off, width, col in (
            (0, WIDE, g * WIDE),
            (WIDE, STATE, INNER + g * STATE),
            (WIDE + STATE, STATE, INNER + (GROUPS + g) * STATE),
        ):
            gtap[0, :, col : col + width] = final[c, j, 0:CONV, off : off + width]
            gcb[0:1, col : col + width] = final[c, j, CONV : CONV + 1, off : off + width]
    for at, ref in enumerate((gsb, gdl, gsk)):
        ref[...] = final[0, HALF, at : at + 1, 0:HEADS] + final[1, HALF, at : at + 1, 0:HEADS]

    @pl.when(sec == 0)
    def _():
        pltpu.make_async_copy(zeros, nxt.at[0, 0], zero_sem.at[0]).wait()

    @pl.when(sec > 0)
    def _():
        low = sec - 1
        remote(stage_c, stage_c, conv_sem.at[0], conv_sem.at[1], core, low, dp).wait_send()
        half_o = stage_o.at[:, :, pl.ds(0, WIDE)]
        remote(half_o, half_o, gate_sem.at[0], gate_sem.at[1], core, low, dp).wait_send()
        remote(stage_s, stage_s, dstep_sem.at[2], dstep_sem.at[0], core, low, dp).wait_send()
        remote(
            nxt.at[0, 0], nxt.at[0, 0], next_sem.at[0], next_sem.at[1], core, low, dp
        ).wait_recv()

    @pl.when(sec == nsec - 1)
    def _():
        whole = gconv.at[0, 0]
        pltpu.make_async_copy(whole, whole, zero_sem.at[1]).wait()
        pltpu.make_async_copy(zeros, ggate.at[0, 0], zero_sem.at[2]).wait()
        gstep[...] = jnp.zeros_like(gstep)

    @pl.when(sec < nsec - 1)
    def _():
        high = sec + 1
        half_o = stage_o.at[:, :, pl.ds(0, WIDE)]
        remote(half_o, half_o, next_sem.at[0], next_sem.at[1], core, high, dp).wait_send()
        for c in range(2):
            part = step_parts.at[c]
            remote(part, part, dstep_sem.at[2], dstep_sem.at[c], core, high, dp).wait_recv()
        gstep[0, 0] = (step_parts[0].astype(F32) + step_parts[1].astype(F32))[:, 0:HEADS].astype(BF16)
        whole = ggate.at[0, 0]
        remote(whole, whole, gate_sem.at[0], gate_sem.at[1], core, high, dp).wait_recv()
        whole = gconv.at[0, 0]
        remote(whole, whole, conv_sem.at[0], conv_sem.at[1], core, high, dp).wait_recv()


def paired(
    conv_input, gate_input, step_input, cotangent, conv_weight,
    conv_bias, step_bias, decay_log, skip_gain, norm_gain,
):
    tok = conv_input.shape[2]
    seq = 2 * tok
    ndp = lax.axis_size("dp")
    hbm = pl.BlockSpec(memory_space=pl.ANY)
    vmem = pl.BlockSpec(memory_space=pltpu.VMEM)
    like = lambda a, kind: jax.ShapeDtypeStruct(a.shape, kind)
    scratch = [
        pltpu.VMEM((HALF, seq, MIX + 2 * WIDE), BF16),
        pltpu.VMEM((2, tok, HEADS), BF16),
        pltpu.VMEM((seq + 8, MIX), F32),
        pltpu.VMEM((seq + 8, MIX), F32),
        pltpu.VMEM((seq, MIX), F32),
        pltpu.VMEM((seq, MIX), F32),
        pltpu.VMEM((seq, 128), F32),
        pltpu.VMEM((seq, 128), F32),
        pltpu.VMEM((seq, 128), F32),
        pltpu.VMEM((seq, 128), F32),
        pltpu.VMEM((128, seq), F32),
        pltpu.VMEM((seq, 128), F32),
        pltpu.VMEM((seq, 128), F32),
        pltpu.VMEM((8, 128), F32),
        pltpu.VMEM((HALF, seq, MIX), BF16),
        pltpu.VMEM((HALF, seq, 2 * WIDE), BF16),
        pltpu.VMEM((seq, 128), BF16),
        pltpu.VMEM((2, tok, 128), BF16),
        pltpu.VMEM((ndp, HALF + 1, 8, MIX), F32),
        pltpu.VMEM((2, HALF + 1, 8, MIX), F32),
        pltpu.VMEM((tok, INNER), BF16),
        pltpu.SemaphoreType.DMA((HALF,)),
        pltpu.SemaphoreType.DMA((HALF,)),
        pltpu.SemaphoreType.DMA((HALF,)),
        pltpu.SemaphoreType.DMA((3,)),
        pltpu.SemaphoreType.DMA((2,)),
        pltpu.SemaphoreType.DMA((2,)),
        pltpu.SemaphoreType.DMA((2,)),
        pltpu.SemaphoreType.DMA((3,)),
        pltpu.SemaphoreType.DMA((ndp,)),
        pltpu.SemaphoreType.DMA((ndp,)),
        pltpu.SemaphoreType.DMA((2,)),
        pltpu.SemaphoreType.DMA((3,)),
    ]
    return tuple(
        pl.pallas_call(
            pair_kernel,
            name="mixer_tick",
            in_specs=[hbm] * 4 + [vmem] * 6,
            out_specs=[hbm] * 3 + [vmem] * 7,
            out_shape=[
                like(gate_input, BF16),
                like(conv_input, BF16),
                like(gate_input, BF16),
                like(step_input, BF16),
                like(conv_weight, F32),
                like(conv_bias, F32),
                like(step_bias, F32),
                like(decay_log, F32),
                like(skip_gain, F32),
                like(norm_gain, F32),
            ],
            scratch_shapes=scratch,
            compiler_params=pltpu.CompilerParams(collective_id=0, has_side_effects=True),
        )(
            conv_input, gate_input, step_input, cotangent, conv_weight,
            conv_bias, step_bias, decay_log, skip_gain, norm_gain,
        )
    )


def solution(mesh):
    in_specs = (
        P("section", "dp", "ctx", None),
        P("section", "dp", "ctx", None),
        P("section", "dp", "ctx", None),
        P("section", "dp", "ctx", None),
        P("section", None, None),
        P("section", None),
        P("section", None),
        P("section", None),
        P("section", None),
        P("section", None),
    )
    out_specs = (
        P("section", "dp", "ctx", None),
        P("section", "dp", "ctx", None),
        P("section", "dp", "ctx", None),
        P("section", "dp", "ctx", None),
        P("section", None, None),
        P("section", None),
        P("section", None),
        P("section", None),
        P("section", None),
        P("section", None),
    )
    body = paired if mesh.shape["ctx"] == 2 else shards
    return jax.shard_map(body, mesh=mesh, in_specs=in_specs, out_specs=out_specs, check_vma=False)
```

profile of v0, /device:TPU:0, one launch (start us, length us, event | category | flops | bytes accessed | tf_op | source)
XLA Modules:
  0.0 64.8 jit_solution(2101429349529123689)
XLA Ops:
  0.6 1.4 %copy.20.step_in = bf16[1,1,128,16]{3,2,1,0:T(8,128)(2,1)} copy(bf16[1,1,128,16]{2,3,1,0:T(8,128)(2,1)} %param.12) | data formatting | bytes 8192 | tf_op args[2]
  2.0 53.0 %mixer_tick.1 = (bf16[1,1,128,1024]{3,2,1,0:T(8,128)(2,1)}, bf16[1,1,128,5120]{3,2,1,0:T(8,128)(2,1)}, bf16[1,1,128,1024]{3,2,1,0:T(8,128)(2,1)}, bf16[1,1,128,1...) custom-call(bf16[1,1,128,5120]{3,2,1,0:T(8,128)(2,1)} %conv_in.1, ...), custom_call_target="tpu_custom_call" | custom-call | tf_op jit(solution)/shard_map/mixer_tick/pallas_call | solution.py:643
  55.1 1.4 %copy.21 = bf16[1,1,128,16]{2,3,1,0:T(8,128)(2,1)} copy(bf16[1,1,128,16]{3,2,1,0:T(8,128)(2,1)} %get-tuple-element.13) | data formatting | bytes 8192 | tf_op jit(solution)/shard_map/mixer_tick/pallas_call | solution.py:643
  56.5 1.7 %copy.31 = bf16[1,1,128,1024]{3,2,1,0:T(8,128)(2,1)} copy(bf16[1,1,128,1024]{3,2,1,0:T(8,128)(2,1)} %get-tuple-element.30) | data formatting | bytes 524288
  58.2 0.0 copy-start
  58.2 0.0 copy-start.1
  58.2 0.0 copy-start.5
  58.2 0.0 copy-start.4
  58.2 0.0 copy-start.3
  58.2 2.5 %copy.32 = bf16[1,1,128,5120]{3,2,1,0:T(8,128)(2,1)} copy(bf16[1,1,128,5120]{3,2,1,0:T(8,128)(2,1)} %get-tuple-element.31) | data formatting | bytes 2621440
  60.7 0.0 copy-done
  60.7 0.7 %copy.33 = bf16[1,1,128,1024]{3,2,1,0:T(8,128)(2,1)} copy(bf16[1,1,128,1024]{3,2,1,0:T(8,128)(2,1)S(1)} %copy-done) | data formatting | bytes 524288
  61.4 0.0 copy-done.1
  61.4 0.6 copy.34
  62.1 0.0 copy-done.2
  62.1 0.6 copy.35
  62.7 0.0 copy-done.6
  62.7 0.5 copy.36
  63.2 0.0 copy-done.5
  63.2 0.5 copy.37
  63.7 0.0 copy-done.4
  63.7 0.5 copy.38
  64.2 0.0 copy-done.3
  64.2 0.6 copy.39
  (2 shorter events, 0.0 us)
Async XLA Ops:
  58.2 2.5 %copy-start = (bf16[1,1,128,1024]{3,2,1,0:T(8,128)(2,1)S(1)}, bf16[1,1,128,1024]{3,2,1,0:T(8,128)(2,1)}, u32[]{:S(2)}) copy-start(bf16[1,1,128,1024]{3,2,1,0:T(8,128)(2,1)} %get-tuple-element.32) | copy-start | bytes 786436
  58.2 3.2 %copy-start.1 = (f32[1,4,5120]{2,1,0:T(4,128)S(1)}, f32[1,4,5120]{2,1,0:T(4,128)}, u32[]{:S(2)}) copy-start(f32[1,4,5120]{2,1,0:T(4,128)} %get-tuple-element.34) | copy-start | bytes 245764
  58.2 3.9 %copy-start.2 = (f32[1,5120]{1,0:T(1,128)S(1)}, f32[1,5120]{1,0:T(1,128)}, u32[]{:S(2)}) copy-start(f32[1,5120]{1,0:T(1,128)} %get-tuple-element.35) | copy-start | bytes 61444
  58.2 4.5 %copy-start.6 = (f32[1,16]{1,0:T(1,128)S(1)}, f32[1,16]{1,0:T(1,128)}, u32[]{:S(2)}) copy-start(f32[1,16]{1,0:T(1,128)} %get-tuple-element.36) | copy-start | bytes 196
  58.2 5.0 %copy-start.5 = (f32[1,16]{1,0:T(1,128)S(1)}, f32[1,16]{1,0:T(1,128)}, u32[]{:S(2)}) copy-start(f32[1,16]{1,0:T(1,128)} %get-tuple-element.37) | copy-start | bytes 196
  58.2 5.5 %copy-start.4 = (f32[1,16]{1,0:T(1,128)S(1)}, f32[1,16]{1,0:T(1,128)}, u32[]{:S(2)}) copy-start(f32[1,16]{1,0:T(1,128)} %get-tuple-element.38) | copy-start | bytes 196
  58.2 6.0 %copy-start.3 = (f32[1,1024]{1,0:T(1,128)S(1)}, f32[1,1024]{1,0:T(1,128)}, u32[]{:S(2)}) copy-start(f32[1,1024]{1,0:T(1,128)} %get-tuple-element.39) | copy-start | bytes 12292
where the time goes:
time: 65.1 us; the launch traced here: 64.8 us
  Pallas kernels  53 us (81%)
  local copies, waits for them, and re-layouts  11.1 us (17%)
  between operations  0.69 us (1%)
    pallas_call x1, Pallas kernels, paired(): pl.pallas_call(pair_kernel, name='mixer_tick', in_specs=[hbm] * 4 + [vmem...  53 us
    unnamed x24, local copies, waits for them, and re-layouts  9.67 us
    pallas_call x1, local copies, waits for them, and re-layouts, paired(): pl.pallas_call(pair_kernel, name='mixer_tick', in_specs=[hbm] * 4 + [vmem...  1.42 us

commit v1 on v0

--- a/solution.py
+++ b/solution.py
@@ -255,8 +255,8 @@
 
 def pair_kernel(
     conv_in, gate_in, step_in, cot_in, w_ref, b_ref, sb_ref, dl_ref, sk_ref, ng_ref,
-    nxt, gconv, ggate, gstep, gtap, gcb, gsb, gdl, gsk, gng,
-    uin, steps, upad, zpad, mix, dsl, dtc, sigc, ratec, cumc, cumr, ddt, drate, small,
+    nxt, gconv, ggate, gstep, packed,
+    uin, steps, steprow, upad, zpad, mix, dsl, dtc, sigc, ratec, cumc, cumr, ddt, drate, small,
     stage_c, stage_o, stage_s, step_parts, partial, final, zeros,
     own_sem, xs_sem, xr_sem, st_sem, conv_sem, gate_sem, next_sem, dstep_sem,
     ps_sem, pr_sem, fin_sem, zero_sem,
@@ -320,7 +320,7 @@
     partial[dp] = jnp.zeros(partial.shape[1:], F32)
     upad[0:8, :] = jnp.zeros((8, MIX), F32)
     zpad[seq : seq + 8, :] = jnp.zeros((8, MIX), F32)
-    for ref in (dtc, sigc, ratec, ddt, drate, small):
+    for ref in (steprow, dtc, sigc, ratec, ddt, drate, small):
         ref[...] = jnp.zeros_like(ref)
     pl.semaphore_wait(barrier, 1 + 4 + (ndp - 1))
     step_copy = remote(
@@ -351,7 +351,9 @@
 
     own_step.wait()
     step_copy.wait()
-    raw = steps[...].astype(F32).reshape(seq, HEADS) + sb_ref[...]
+    for c in range(2):
+        steprow[0:HEADS, c * tok : (c + 1) * tok] = steps[c].astype(F32)
+    raw = steprow[...].T[:, 0:HEADS] + sb_ref[...]
     delta = jnp.maximum(raw, 0.0) + jnp.log1p(jnp.exp(-jnp.abs(raw)))
     dtc[:, 0:HEADS] = delta
     sigc[:, 0:HEADS] = jax.nn.sigmoid(raw)
@@ -453,55 +455,57 @@
         partial[dp, j, 5:6, 0:WIDE] = jnp.sum(cot * normed, axis=0, keepdims=True)
         dyx = jnp.sum(dy * x, axis=0, keepdims=True)
         dscore = jnp.zeros((seq, seq), F32)
-        dxs = []
-        upper = jnp.where(row <= column, 1.0, 0.0).astype(BF16)
         dy_p = split(dy)
+        das = []
         for r in range(REPS):
             own = first if r == 0 else jnp.logical_not(first)
-            dyr_p = split(jnp.where(own, dy, 0.0))
-            da = dot3(dyr_p, xs_p, NT)
+            da = dot3(split(jnp.where(own, dy, 0.0)), xs_p, NT)
+            das.append(da)
             dscore = dscore + da * decay[r]
-            p = split(da * mixed[r][0])
+        ds_p = split(dscore)
+
+        def conv_back(off, width, start):
+            for part in range(width // 128):
+                here = slice(off + part * 128, off + part * 128 + 128)
+                col = pl.multiple_of(start + part * 128, 128)
+                dz = zpad[0:seq, here]
+                du = jnp.zeros((seq, 128), F32)
+                for k in range(CONV):
+                    du = du + w_ref[0, pl.ds(k, 1), pl.ds(col, 128)] * zpad[3 - k : 3 - k + seq, here]
+                    partial[dp, j, pl.ds(k, 1), here] = jnp.sum(
+                        dz * upad[5 + k : 5 + k + seq, here], axis=0, keepdims=True
+                    )
+                partial[dp, j, pl.ds(4, 1), here] = jnp.sum(dz, axis=0, keepdims=True)
+                stage_c[j, :, here] = du.astype(BF16)
+
+            @pl.when(sec > 0)
+            def _():
+                for t in range(2):
+                    remote(
+                        stage_c.at[j, pl.ds(t * tok, tok), pl.ds(off, width)],
+                        gconv.at[0, 0, :, pl.ds(start, width)],
+                        conv_sem.at[0], conv_sem.at[1], t, sec - 1, dp,
+                    ).start()
+
+        zpad[0:seq, WIDE + STATE : MIX] = dot3(ds_p, bmap, NN) * dsl[:, WIDE + STATE : MIX]
+        conv_back(WIDE + STATE, STATE, cols[2])
+        zpad[0:seq, WIDE : WIDE + STATE] = dot3(ds_p, cmap, TN) * dsl[:, WIDE : WIDE + STATE]
+        conv_back(WIDE, STATE, cols[1])
+        dxs = jnp.where(first, dot3(mixed[0][1], dy_p, TN), dot3(mixed[1][1], dy_p, TN))
+        zpad[0:seq, 0:WIDE] = (skip2 * dy + dxs * dt2) * dsl[:, 0:WIDE]
+        conv_back(0, WIDE, cols[0])
+        upper = jnp.where(row <= column, 1.0, 0.0).astype(BF16)
+        dxx = dxs * x
+        for r in range(REPS):
+            own = first if r == 0 else jnp.logical_not(first)
+            p = split(das[r] * mixed[r][0])
             later = dot(upper, p[0], NN) + dot(upper, p[1], NN)
             dr = jnp.sum(jnp.where(row > column, later, 0.0), axis=1, keepdims=True)
             drate[...] += jnp.where(lane == h0 + r, dr, 0.0)
-            dxs.append(dot3(mixed[r][1], dy_p, TN))
             total = jnp.sum(jnp.where(own[0:1], dyx, 0.0), axis=1, keepdims=True)
             small[2:3, :] += jnp.where(lane1 == h0 + r, total, 0.0)
-        dxs = jnp.where(first, dxs[0], dxs[1])
-        dxx = dxs * x
-        ddt[...] += jnp.where(
-            lane == h0, jnp.sum(jnp.where(first, dxx, 0.0), axis=1, keepdims=True), 0.0
-        ) + jnp.where(
-            lane == h0 + 1, jnp.sum(jnp.where(first, 0.0, dxx), axis=1, keepdims=True), 0.0
-        )
-        ds_p = split(dscore)
-        zpad[0:seq, 0:WIDE] = (skip2 * dy + dxs * dt2) * dsl[:, 0:WIDE]
-        zpad[0:seq, WIDE : WIDE + STATE] = dot3(ds_p, cmap, TN) * dsl[:, WIDE : WIDE + STATE]
-        zpad[0:seq, WIDE + STATE : MIX] = dot3(ds_p, bmap, NN) * dsl[:, WIDE + STATE : MIX]
-        for off, col in blocks:
-            here = slice(off, off + 128)
-            dz = zpad[0:seq, here]
-            du = jnp.zeros((seq, 128), F32)
-            for k in range(CONV):
-                du = du + w_ref[0, pl.ds(k, 1), pl.ds(col, 128)] * zpad[3 - k : 3 - k + seq, here]
-                partial[dp, j, pl.ds(k, 1), here] = jnp.sum(
-                    dz * upad[5 + k : 5 + k + seq, here], axis=0, keepdims=True
-                )
-            partial[dp, j, pl.ds(4, 1), here] = jnp.sum(dz, axis=0, keepdims=True)
-            stage_c[j, :, here] = du.astype(BF16)
-
-        @pl.when(sec > 0)
-        def _():
-            for t in range(2):
-                for off, width, col in (
-                    (0, WIDE, cols[0]), (WIDE, STATE, cols[1]), (WIDE + STATE, STATE, cols[2])
-                ):
-                    remote(
-                        stage_c.at[j, pl.ds(t * tok, tok), pl.ds(off, width)],
-                        gconv.at[0, 0, :, pl.ds(col, width)],
-                        conv_sem.at[0], conv_sem.at[1], t, sec - 1, dp,
-                    ).start()
+            dd = jnp.sum(jnp.where(own, dxx, 0.0), axis=1, keepdims=True)
+            ddt[...] += jnp.where(lane == h0 + r, dd, 0.0)
 
         for k in range(1, ndp):
             to = lax.rem(dp + k, ndp)
@@ -517,14 +521,16 @@
     dstep = (ddt[:, 0:HEADS] - dr16 * damp) * sigc[:, 0:HEADS]
     small[0:1, 0:HEADS] = jnp.sum(dstep, axis=0, keepdims=True)
     small[1:2, 0:HEADS] = jnp.sum(dr16 * ratec[:, 0:HEADS], axis=0, keepdims=True)
-    stage_s[...] = jnp.zeros_like(stage_s)
-    stage_s[:, 0:HEADS] = dstep.astype(BF16)
+    drate[:, 0:HEADS] = dstep
+    turned = drate[...].T
+    for t in range(2):
+        stage_s[t] = turned[0:HEADS, t * tok : (t + 1) * tok].astype(BF16)
 
     @pl.when(sec > 0)
     def _():
         for t in range(2):
             remote(
-                stage_s.at[pl.ds(t * tok, tok)], step_parts.at[core],
+                stage_s.at[t], step_parts.at[core],
                 dstep_sem.at[2], dstep_sem.at[core], t, sec - 1, dp,
             ).start()
 
@@ -544,18 +550,7 @@
     halves = remote(final.at[core], final.at[core], fin_sem.at[0], fin_sem.at[1], other, sec, dp)
     halves.start()
     remote(final.at[core], final.at[other], fin_sem.at[0], fin_sem.at[1], other, sec, dp).wait()
-    for g in range(GROUPS):
-        c, j = g // HALF, g % HALF
-        gng[0:1, g * WIDE : (g + 1) * WIDE] = final[c, j, 5:6, 0:WIDE]
-        for off, width, col in (
-            (0, WIDE, g * WIDE),
-            (WIDE, STATE, INNER + g * STATE),
-            (WIDE + STATE, STATE, INNER + (GROUPS + g) * STATE),
-        ):
-            gtap[0, :, col : col + width] = final[c, j, 0:CONV, off : off + width]
-            gcb[0:1, col : col + width] = final[c, j, CONV : CONV + 1, off : off + width]
-    for at, ref in enumerate((gsb, gdl, gsk)):
-        ref[...] = final[0, HALF, at : at + 1, 0:HEADS] + final[1, HALF, at : at + 1, 0:HEADS]
+    packed[...] = final[...]
 
     @pl.when(sec == 0)
     def _():
@@ -587,11 +582,44 @@
         for c in range(2):
             part = step_parts.at[c]
             remote(part, part, dstep_sem.at[2], dstep_sem.at[c], core, high, dp).wait_recv()
-        gstep[0, 0] = (step_parts[0].astype(F32) + step_parts[1].astype(F32))[:, 0:HEADS].astype(BF16)
+        gstep[0, 0] = (step_parts[0].astype(F32) + step_parts[1].astype(F32)).astype(BF16)
         whole = ggate.at[0, 0]
         remote(whole, whole, gate_sem.at[0], gate_sem.at[1], core, high, dp).wait_recv()
         whole = gconv.at[0, 0]
         remote(whole, whole, conv_sem.at[0], conv_sem.at[1], core, high, dp).wait_recv()
+
+
+def finish_kernel(
+    nxt_in, gconv_in, ggate_in, gstep_in, packed,
+    nxt, gconv, ggate, gstep, gtap, gcb, gsb, gdl, gsk, gng,
+    held, in_sem, out_sem,
+):
+    routes = [(nxt_in.at[0, 0], nxt.at[0, 0]), (ggate_in.at[0, 0], ggate.at[0, 0])]
+    for part in range(5):
+        cut = pl.ds(part * INNER, INNER)
+        routes.append((gconv_in.at[0, 0, :, cut], gconv.at[0, 0, :, cut]))
+    arrive = [pltpu.make_async_copy(r[0], held.at[i], in_sem.at[i]) for i, r in enumerate(routes)]
+    leave = [pltpu.make_async_copy(held.at[i], r[1], out_sem.at[i]) for i, r in enumerate(routes)]
+    for copy in arrive:
+        copy.start()
+    gstep[...] = gstep_in[...]
+    for g in range(GROUPS):
+        c, j = g // HALF, g % HALF
+        gng[0:1, g * WIDE : (g + 1) * WIDE] = packed[c, j, 5:6, 0:WIDE]
+        for off, width, col in (
+            (0, WIDE, g * WIDE),
+            (WIDE, STATE, INNER + g * STATE),
+            (WIDE + STATE, STATE, INNER + (GROUPS + g) * STATE),
+        ):
+            gtap[0, :, col : col + width] = packed[c, j, 0:CONV, off : off + width]
+            gcb[0:1, col : col + width] = packed[c, j, CONV : CONV + 1, off : off + width]
+    for at, ref in enumerate((gsb, gdl, gsk)):
+        ref[...] = packed[0, HALF, at : at + 1, 0:HEADS] + packed[1, HALF, at : at + 1, 0:HEADS]
+    for into, out in zip(arrive, leave):
+        into.wait()
+        out.start()
+    for out in leave:
+        out.wait()
 
 
 def paired(
@@ -606,7 +634,8 @@
     like = lambda a, kind: jax.ShapeDtypeStruct(a.shape, kind)
     scratch = [
         pltpu.VMEM((HALF, seq, MIX + 2 * WIDE), BF16),
-        pltpu.VMEM((2, tok, HEADS), BF16),
+        pltpu.VMEM((2, HEADS, tok), BF16),
+        pltpu.VMEM((128, seq), F32),
         pltpu.VMEM((seq + 8, MIX), F32),
         pltpu.VMEM((seq + 8, MIX), F32),
         pltpu.VMEM((seq, MIX), F32),
@@ -621,8 +650,8 @@
         pltpu.VMEM((8, 128), F32),
         pltpu.VMEM((HALF, seq, MIX), BF16),
         pltpu.VMEM((HALF, seq, 2 * WIDE), BF16),
-        pltpu.VMEM((seq, 128), BF16),
-        pltpu.VMEM((2, tok, 128), BF16),
+        pltpu.VMEM((2, HEADS, tok), BF16),
+        pltpu.VMEM((2, HEADS, tok), BF16),
         pltpu.VMEM((ndp, HALF + 1, 8, MIX), F32),
         pltpu.VMEM((2, HALF + 1, 8, MIX), F32),
         pltpu.VMEM((tok, INNER), BF16),
@@ -639,31 +668,49 @@
         pltpu.SemaphoreType.DMA((2,)),
         pltpu.SemaphoreType.DMA((3,)),
     ]
-    return tuple(
-        pl.pallas_call(
-            pair_kernel,
-            name="mixer_tick",
-            in_specs=[hbm] * 4 + [vmem] * 6,
-            out_specs=[hbm] * 3 + [vmem] * 7,
-            out_shape=[
-                like(gate_input, BF16),
-                like(conv_input, BF16),
-                like(gate_input, BF16),
-                like(step_input, BF16),
-                like(conv_weight, F32),
-                like(conv_bias, F32),
-                like(step_bias, F32),
-                like(decay_log, F32),
-                like(skip_gain, F32),
-                like(norm_gain, F32),
-            ],
-            scratch_shapes=scratch,
-            compiler_params=pltpu.CompilerParams(collective_id=0, has_side_effects=True),
-        )(
-            conv_input, gate_input, step_input, cotangent, conv_weight,
-            conv_bias, step_bias, decay_log, skip_gain, norm_gain,
-        )
-    )
+    turned = jnp.swapaxes(step_input, 2, 3)
+    sent = pl.pallas_call(
+        pair_kernel,
+        name="mixer_tick",
+        in_specs=[hbm] * 4 + [vmem] * 6,
+        out_specs=[hbm] * 3 + [vmem] * 2,
+        out_shape=[
+            like(gate_input, BF16),
+            like(conv_input, BF16),
+            like(gate_input, BF16),
+            like(turned, BF16),
+            jax.ShapeDtypeStruct((2, HALF + 1, 8, MIX), F32),
+        ],
+        scratch_shapes=scratch,
+        compiler_params=pltpu.CompilerParams(collective_id=0, has_side_effects=True),
+    )(
+        conv_input, gate_input, turned, cotangent, conv_weight,
+        conv_bias, step_bias, decay_log, skip_gain, norm_gain,
+    )
+    done = pl.pallas_call(
+        finish_kernel,
+        name="mixer_finish",
+        in_specs=[hbm] * 3 + [vmem] * 2,
+        out_specs=[hbm] * 3 + [vmem] * 7,
+        out_shape=[
+            like(gate_input, BF16),
+            like(conv_input, BF16),
+            like(gate_input, BF16),
+            like(turned, BF16),
+            like(conv_weight, F32),
+            like(conv_bias, F32),
+            like(step_bias, F32),
+            like(decay_log, F32),
+            like(skip_gain, F32),
+            like(norm_gain, F32),
+        ],
+        scratch_shapes=[
+            pltpu.VMEM((7, tok, INNER), BF16),
+            pltpu.SemaphoreType.DMA((7,)),
+            pltpu.SemaphoreType.DMA((7,)),
+        ],
+    )(*sent)
+    return tuple(done[:3]) + (jnp.swapaxes(done[3], 2, 3),) + tuple(done[4:])
 
 
 def solution(mesh):

time: 65.1 us -> 56.9 us (0.87)
  local copies, waits for them, and re-layouts: 11.1 us -> 0 us
  Pallas kernels: 53 us -> 56 us
    unnamed x24 -> x0, local copies, waits for them, and re-layouts: 9.67 us -> none
    pallas_call x0 -> x1, Pallas kernels: none -> 3.88 us  [paired(): pl.pallas_call(finish_kernel, name='mixer_finish', in_specs=[hbm] * 3 + [...]
    pallas_call x1 -> x0, local copies, waits for them, and re-layouts: 1.42 us -> none  [paired(): pl.pallas_call(pair_kernel, name='mixer_tick', in_specs=[hbm] * 4 + [vmem...]
    pallas_call x1, Pallas kernels: 53 us -> 52.1 us  [paired(): pl.pallas_call(pair_kernel, name='mixer_tick', in_specs=[hbm] * 4 + [vmem...]
where the time goes in v1:
time: 56.9 us; the launch traced here: 56.7 us
  Pallas kernels  56 us (98%)
  between operations  0.65 us (1%)
    pallas_call x1, Pallas kernels, paired(): pl.pallas_call(pair_kernel, name='mixer_tick', in_specs=[hbm] * 4 + [vmem...  52.1 us
    pallas_call x1, Pallas kernels, paired(): pl.pallas_call(finish_kernel, name='mixer_finish', in_specs=[hbm] * 3 + [...  3.88 us

profile of v1, /device:TPU:0, one launch (start us, length us, event | category | flops | bytes accessed | tf_op | source)
XLA Modules:
  0.0 56.7 jit_solution(7147494406758872850)
XLA Ops:
  0.6 52.1 %mixer_tick.1 = (bf16[1,1,128,1024]{3,2,1,0:T(8,128)(2,1)}, bf16[1,1,128,5120]{3,2,1,0:T(8,128)(2,1)}, bf16[1,1,128,1024]{3,2,1,0:T(8,128)(2,1)}, bf16[1,1,16,128]{3,2,1,0:T(8,128)(2,1)}, f32[2,5,8,640]{3,2,1,0:T(8,128)}) custom-call(bf16[1,1,128,5120]{3,2,1,0:T(8,128)(2,1)} %conv_in.1, bf16[1,1,128,1024]{3,2,1,0:T(8,128)(2,1)} %gate_in.1, ...), custom_call_target="tpu_custom_call" | custom-call | tf_op jit(solution)/shard_map/mixer_tick/pallas_call | solution.py:672
  52.8 3.9 %mixer_finish.1 = (bf16[1,1,128,1024]{3,2,1,0:T(8,128)(2,1)}, bf16[1,1,128,5120]{3,2,1,0:T(8,128)(2,1)}, bf16[1,1,128,1024]{3,2,1,0:T(8,128)(2,1)}, bf16[1,1,16,...) custom-call(bf16[1,1,128,1024]{3,2,1,0:T(8,128)(2,1)} %get-tuple-ele, ...), custom_call_target="tpu_custom_call" | custom-call | tf_op jit(solution)/shard_map/mixer_finish/pallas_call | solution.py:690

commit v2 on v1

--- a/solution.py
+++ b/solution.py
@@ -257,9 +257,9 @@
     conv_in, gate_in, step_in, cot_in, w_ref, b_ref, sb_ref, dl_ref, sk_ref, ng_ref,
     nxt, gconv, ggate, gstep, packed,
     uin, steps, steprow, upad, zpad, mix, dsl, dtc, sigc, ratec, cumc, cumr, ddt, drate, small,
-    stage_c, stage_o, stage_s, step_parts, partial, final, zeros,
+    stage_c, stage_o, stage_s, step_parts, partial, final, zeros, relay,
     own_sem, xs_sem, xr_sem, st_sem, conv_sem, gate_sem, next_sem, dstep_sem,
-    ps_sem, pr_sem, fin_sem, zero_sem,
+    ps_sem, pr_sem, fin_sem, zero_sem, via_sem, relay_sem,
 ):
     core = lax.axis_index("ctx")
     sec = lax.axis_index("section")
@@ -290,6 +290,7 @@
     for c in range(2):
         greet(c, after, dp)
         greet(c, before, dp)
+        greet(c, lax.rem(sec + 2, nsec), dp)
     for k in range(1, ndp):
         greet(core, sec, lax.rem(dp + k, ndp))
 
@@ -322,7 +323,7 @@
     zpad[seq : seq + 8, :] = jnp.zeros((8, MIX), F32)
     for ref in (steprow, dtc, sigc, ratec, ddt, drate, small):
         ref[...] = jnp.zeros_like(ref)
-    pl.semaphore_wait(barrier, 1 + 4 + (ndp - 1))
+    pl.semaphore_wait(barrier, 1 + 6 + (ndp - 1))
     step_copy = remote(
         step_in.at[0, 0], steps.at[core], st_sem.at[1], st_sem.at[2], other, sec, dp
     )
@@ -434,23 +435,40 @@
         dy = dgated * act
         stage_o[j, :, WIDE : 2 * WIDE] = (dgated * y * (s * (1.0 + gate * (1.0 - s)))).astype(BF16)
 
-        @pl.when(sec < nsec - 1)
+        odd = lax.rem(j, 2) == 1
+
+        def send_half(base, t, dst, done, landed, s):
+            remote(
+                stage_o.at[j, pl.ds(t * tok, tok), pl.ds(base, WIDE)], dst, done, landed, t, s, dp
+            ).start()
+
+        @pl.when(jnp.logical_and(sec < nsec - 1, jnp.logical_not(jnp.logical_and(sec == 1, odd))))
         def _():
             for t in range(2):
-                remote(
-                    stage_o.at[j, pl.ds(t * tok, tok), pl.ds(0, WIDE)],
-                    nxt.at[0, 0, :, pl.ds(cols[0], WIDE)],
-                    next_sem.at[0], next_sem.at[1], t, sec + 1, dp,
-                ).start()
-
-        @pl.when(sec > 0)
+                send_half(
+                    0, t, nxt.at[0, 0, :, pl.ds(cols[0], WIDE)],
+                    next_sem.at[0], next_sem.at[1], sec + 1,
+                )
+
+        @pl.when(jnp.logical_and(sec == 1, odd))
+        def _():
+            slot = core * (HALF // 2) + j // 2
+            for t in range(2):
+                send_half(0, t, relay.at[slot], next_sem.at[0], relay_sem.at[slot], 3)
+
+        @pl.when(jnp.logical_or(sec == 1, sec == 3))
         def _():
             for t in range(2):
-                remote(
-                    stage_o.at[j, pl.ds(t * tok, tok), pl.ds(WIDE, WIDE)],
-                    ggate.at[0, 0, :, pl.ds(cols[0], WIDE)],
-                    gate_sem.at[0], gate_sem.at[1], t, sec - 1, dp,
-                ).start()
+                send_half(
+                    WIDE, t, ggate.at[0, 0, :, pl.ds(cols[0], WIDE)],
+                    gate_sem.at[0], gate_sem.at[1], sec - 1,
+                )
+
+        @pl.when(sec == 2)
+        def _():
+            slot = core * HALF + j
+            for t in range(2):
+                send_half(WIDE, t, relay.at[slot], gate_sem.at[0], relay_sem.at[slot], 0)
 
         partial[dp, j, 5:6, 0:WIDE] = jnp.sum(cot * normed, axis=0, keepdims=True)
         dyx = jnp.sum(dy * x, axis=0, keepdims=True)
@@ -516,6 +534,23 @@
 
     lax.fori_loop(0, HALF, group, 0)
 
+    def pass_on(slot, g, out, landed, s):
+        part = relay.at[slot]
+        remote(part, part, via_sem.at[0], relay_sem.at[slot], core, s, dp).wait_recv()
+        remote(
+            part, out.at[0, 0, :, pl.ds(g * WIDE, WIDE)], via_sem.at[0], landed, core, s, dp
+        ).start()
+
+    @pl.when(sec == 0)
+    def _():
+        for g in range(GROUPS):
+            pass_on(g, g, ggate, gate_sem.at[1], 1)
+
+    @pl.when(sec == 3)
+    def _():
+        for at in range(GROUPS // 2):
+            pass_on(at, 2 * at + 1, nxt, next_sem.at[1], 2)
+
     damp = jnp.exp(dl_ref[...])
     dr16 = drate[:, 0:HEADS]
     dstep = (ddt[:, 0:HEADS] - dr16 * damp) * sigc[:, 0:HEADS]
@@ -555,6 +590,7 @@
     @pl.when(sec == 0)
     def _():
         pltpu.make_async_copy(zeros, nxt.at[0, 0], zero_sem.at[0]).wait()
+        remote(relay, relay, via_sem.at[0], relay_sem.at[0], core, 1, dp).wait_send()
 
     @pl.when(sec > 0)
     def _():
@@ -573,6 +609,8 @@
         pltpu.make_async_copy(whole, whole, zero_sem.at[1]).wait()
         pltpu.make_async_copy(zeros, ggate.at[0, 0], zero_sem.at[2]).wait()
         gstep[...] = jnp.zeros_like(gstep)
+        used = relay.at[pl.ds(0, GROUPS // 2)]
+        remote(used, used, via_sem.at[0], relay_sem.at[0], core, 2, dp).wait_send()
 
     @pl.when(sec < nsec - 1)
     def _():
@@ -655,6 +693,7 @@
         pltpu.VMEM((ndp, HALF + 1, 8, MIX), F32),
         pltpu.VMEM((2, HALF + 1, 8, MIX), F32),
         pltpu.VMEM((tok, INNER), BF16),
+        pltpu.VMEM((GROUPS, tok, WIDE), BF16),
         pltpu.SemaphoreType.DMA((HALF,)),
         pltpu.SemaphoreType.DMA((HALF,)),
         pltpu.SemaphoreType.DMA((HALF,)),
@@ -667,6 +706,8 @@
         pltpu.SemaphoreType.DMA((ndp,)),
         pltpu.SemaphoreType.DMA((2,)),
         pltpu.SemaphoreType.DMA((3,)),
+        pltpu.SemaphoreType.DMA((1,)),
+        pltpu.SemaphoreType.DMA((GROUPS,)),
     ]
     turned = jnp.swapaxes(step_input, 2, 3)
     sent = pl.pallas_call(
@@ -738,5 +779,5 @@
         P("section", None),
         P("section", None),
     )
-    body = paired if mesh.shape["ctx"] == 2 else shards
+    body = paired if (mesh.shape["ctx"], mesh.shape["section"]) == (2, 4) else shards
     return jax.shard_map(body, mesh=mesh, in_specs=in_specs, out_specs=out_specs, check_vma=False)

time: 56.9 us -> 54.1 us (0.951)
  Pallas kernels: 56 us -> 53.3 us
    pallas_call x1, Pallas kernels: 52.1 us -> 49.4 us  [paired(): pl.pallas_call(pair_kernel, name='mixer_tick', in_specs=[hbm] * 4 + [vmem...]
where the time goes in v2:
time: 54.1 us; the launch traced here: 53.9 us
  Pallas kernels  53.3 us (99%)
  between operations  0.65 us (1%)
    pallas_call x1, Pallas kernels, paired(): pl.pallas_call(pair_kernel, name='mixer_tick', in_specs=[hbm] * 4 + [vmem...  49.4 us
    pallas_call x1, Pallas kernels, paired(): pl.pallas_call(finish_kernel, name='mixer_finish', in_specs=[hbm] * 3 + [...  3.88 us

profile of v2, /device:TPU:0, one launch (start us, length us, event | category | flops | bytes accessed | tf_op | source)
XLA Modules:
  0.0 53.9 jit_solution(5380074535597700387)
XLA Ops:
  0.6 49.4 %mixer_tick.1 = (bf16[1,1,128,1024]{3,2,1,0:T(8,128)(2,1)}, bf16[1,1,128,5120]{3,2,1,0:T(8,128)(2,1)}, bf16[1,1,128,1024]{3,2,1,0:T(8,128)(2,1)}, bf16[1,1,16,128]{3,2,1,0:T(8,128)(2,1)}, f32[2,5,8,640]{3,2,1,0:T(8,128)}) custom-call(bf16[1,1,128,5120]{3,2,1,0:T(8,128)(2,1)} %conv_in.1, bf16[1,1,128,1024]{3,2,1,0:T(8,128)(2,1)} %gate_in.1, ...), custom_call_target="tpu_custom_call" | custom-call | tf_op jit(solution)/shard_map/mixer_tick/pallas_call | solution.py:713
  50.1 3.9 %mixer_finish.1 = (bf16[1,1,128,1024]{3,2,1,0:T(8,128)(2,1)}, bf16[1,1,128,5120]{3,2,1,0:T(8,128)(2,1)}, bf16[1,1,128,1024]{3,2,1,0:T(8,128)(2,1)}, bf16[1,1,16,...) custom-call(bf16[1,1,128,1024]{3,2,1,0:T(8,128)(2,1)} %get-tuple-ele, ...), custom_call_target="tpu_custom_call" | custom-call | tf_op jit(solution)/shard_map/mixer_finish/pallas_call | solution.py:731

commit v3 on v2

--- a/solution.py
+++ b/solution.py
@@ -257,7 +257,7 @@
     conv_in, gate_in, step_in, cot_in, w_ref, b_ref, sb_ref, dl_ref, sk_ref, ng_ref,
     nxt, gconv, ggate, gstep, packed,
     uin, steps, steprow, upad, zpad, mix, dsl, dtc, sigc, ratec, cumc, cumr, ddt, drate, small,
-    stage_c, stage_o, stage_s, step_parts, partial, final, zeros, relay,
+    stage_c, stage_o, stage_s, step_parts, partial, final, zeros, relay, step_out,
     own_sem, xs_sem, xr_sem, st_sem, conv_sem, gate_sem, next_sem, dstep_sem,
     ps_sem, pr_sem, fin_sem, zero_sem, via_sem, relay_sem,
 ):
@@ -585,7 +585,22 @@
     halves = remote(final.at[core], final.at[core], fin_sem.at[0], fin_sem.at[1], other, sec, dp)
     halves.start()
     remote(final.at[core], final.at[other], fin_sem.at[0], fin_sem.at[1], other, sec, dp).wait()
-    packed[...] = final[...]
+    to_packed = pltpu.make_async_copy(final, packed, own_sem.at[0])
+    to_packed.start()
+
+    @pl.when(sec == nsec - 1)
+    def _():
+        step_out[...] = jnp.zeros_like(step_out)
+
+    @pl.when(sec < nsec - 1)
+    def _():
+        for c in range(2):
+            part = step_parts.at[c]
+            remote(part, part, dstep_sem.at[2], dstep_sem.at[c], core, sec + 1, dp).wait_recv()
+        step_out[...] = (step_parts[0].astype(F32) + step_parts[1].astype(F32)).astype(BF16)
+
+    to_step = pltpu.make_async_copy(step_out, gstep.at[0, 0], own_sem.at[1])
+    to_step.start()
 
     @pl.when(sec == 0)
     def _():
@@ -608,7 +623,6 @@
         whole = gconv.at[0, 0]
         pltpu.make_async_copy(whole, whole, zero_sem.at[1]).wait()
         pltpu.make_async_copy(zeros, ggate.at[0, 0], zero_sem.at[2]).wait()
-        gstep[...] = jnp.zeros_like(gstep)
         used = relay.at[pl.ds(0, GROUPS // 2)]
         remote(used, used, via_sem.at[0], relay_sem.at[0], core, 2, dp).wait_send()
 
@@ -617,30 +631,38 @@
         high = sec + 1
         half_o = stage_o.at[:, :, pl.ds(0, WIDE)]
         remote(half_o, half_o, next_sem.at[0], next_sem.at[1], core, high, dp).wait_send()
-        for c in range(2):
-            part = step_parts.at[c]
-            remote(part, part, dstep_sem.at[2], dstep_sem.at[c], core, high, dp).wait_recv()
-        gstep[0, 0] = (step_parts[0].astype(F32) + step_parts[1].astype(F32)).astype(BF16)
         whole = ggate.at[0, 0]
         remote(whole, whole, gate_sem.at[0], gate_sem.at[1], core, high, dp).wait_recv()
         whole = gconv.at[0, 0]
         remote(whole, whole, conv_sem.at[0], conv_sem.at[1], core, high, dp).wait_recv()
 
+    to_packed.wait()
+    to_step.wait()
+
 
 def finish_kernel(
-    nxt_in, gconv_in, ggate_in, gstep_in, packed,
+    nxt_in, gconv_in, ggate_in, gstep_in, packed_in,
     nxt, gconv, ggate, gstep, gtap, gcb, gsb, gdl, gsk, gng,
-    held, in_sem, out_sem,
+    held, held_step, packed, in_sem, out_sem,
 ):
-    routes = [(nxt_in.at[0, 0], nxt.at[0, 0]), (ggate_in.at[0, 0], ggate.at[0, 0])]
+    routes = [
+        (gstep_in.at[0, 0], held_step, gstep.at[0, 0]),
+        (nxt_in.at[0, 0], held.at[0], nxt.at[0, 0]),
+        (ggate_in.at[0, 0], held.at[1], ggate.at[0, 0]),
+    ]
     for part in range(5):
         cut = pl.ds(part * INNER, INNER)
-        routes.append((gconv_in.at[0, 0, :, cut], gconv.at[0, 0, :, cut]))
-    arrive = [pltpu.make_async_copy(r[0], held.at[i], in_sem.at[i]) for i, r in enumerate(routes)]
-    leave = [pltpu.make_async_copy(held.at[i], r[1], out_sem.at[i]) for i, r in enumerate(routes)]
+        routes.append((gconv_in.at[0, 0, :, cut], held.at[2 + part], gconv.at[0, 0, :, cut]))
+    arrive = [pltpu.make_async_copy(a, b, in_sem.at[i]) for i, (a, b, _) in enumerate(routes)]
+    leave = [pltpu.make_async_copy(b, c, out_sem.at[i]) for i, (_, b, c) in enumerate(routes)]
+    first = pltpu.make_async_copy(packed_in, packed, in_sem.at[8])
+    first.start()
     for copy in arrive:
         copy.start()
-    gstep[...] = gstep_in[...]
+    for into, out in zip(arrive, leave):
+        into.wait()
+        out.start()
+    first.wait()
     for g in range(GROUPS):
         c, j = g // HALF, g % HALF
         gng[0:1, g * WIDE : (g + 1) * WIDE] = packed[c, j, 5:6, 0:WIDE]
@@ -653,9 +675,6 @@
             gcb[0:1, col : col + width] = packed[c, j, CONV : CONV + 1, off : off + width]
     for at, ref in enumerate((gsb, gdl, gsk)):
         ref[...] = packed[0, HALF, at : at + 1, 0:HEADS] + packed[1, HALF, at : at + 1, 0:HEADS]
-    for into, out in zip(arrive, leave):
-        into.wait()
-        out.start()
     for out in leave:
         out.wait()
 
@@ -694,6 +713,7 @@
         pltpu.VMEM((2, HALF + 1, 8, MIX), F32),
         pltpu.VMEM((tok, INNER), BF16),
         pltpu.VMEM((GROUPS, tok, WIDE), BF16),
+        pltpu.VMEM((HEADS, tok), BF16),
         pltpu.SemaphoreType.DMA((HALF,)),
         pltpu.SemaphoreType.DMA((HALF,)),
         pltpu.SemaphoreType.DMA((HALF,)),
@@ -714,7 +734,7 @@
         pair_kernel,
         name="mixer_tick",
         in_specs=[hbm] * 4 + [vmem] * 6,
-        out_specs=[hbm] * 3 + [vmem] * 2,
+        out_specs=[hbm] * 5,
         out_shape=[
             like(gate_input, BF16),
             like(conv_input, BF16),
@@ -731,8 +751,8 @@
     done = pl.pallas_call(
         finish_kernel,
         name="mixer_finish",
-        in_specs=[hbm] * 3 + [vmem] * 2,
-        out_specs=[hbm] * 3 + [vmem] * 7,
+        in_specs=[hbm] * 5,
+        out_specs=[hbm] * 4 + [vmem] * 6,
         out_shape=[
             like(gate_input, BF16),
             like(conv_input, BF16),
@@ -747,8 +767,10 @@
         ],
         scratch_shapes=[
             pltpu.VMEM((7, tok, INNER), BF16),
-            pltpu.SemaphoreType.DMA((7,)),
-            pltpu.SemaphoreType.DMA((7,)),
+            pltpu.VMEM((HEADS, tok), BF16),
+            pltpu.VMEM((2, HALF + 1, 8, MIX), F32),
+            pltpu.SemaphoreType.DMA((9,)),
+            pltpu.SemaphoreType.DMA((8,)),
         ],
     )(*sent)
     return tuple(done[:3]) + (jnp.swapaxes(done[3], 2, 3),) + tuple(done[4:])

time: 54.1 us -> 53.2 us (0.983)
  Pallas kernels: 53.3 us -> 52.4 us
    pallas_call x1, Pallas kernels: 3.88 us -> 3.08 us  [paired(): pl.pallas_call(finish_kernel, name='mixer_finish', in_specs=[hbm] * 5, ou...]
where the time goes in v3:
time: 53.2 us; the launch traced here: 53 us
  Pallas kernels  52.4 us (98%)
  between operations  0.65 us (1%)
    pallas_call x1, Pallas kernels, paired(): pl.pallas_call(pair_kernel, name='mixer_tick', in_specs=[hbm] * 4 + [vmem...  49.3 us
    pallas_call x1, Pallas kernels, paired(): pl.pallas_call(finish_kernel, name='mixer_finish', in_specs=[hbm] * 5, ou...  3.08 us

profile of v3, /device:TPU:0, one launch (start us, length us, event | category | flops | bytes accessed | tf_op | source)
XLA Modules:
  0.0 53.0 jit_solution(9391551526008003464)
XLA Ops:
  0.6 49.3 %mixer_tick.1 = (bf16[1,1,128,1024]{3,2,1,0:T(8,128)(2,1)}, bf16[1,1,128,5120]{3,2,1,0:T(8,128)(2,1)}, bf16[1,1,128,1024]{3,2,1,0:T(8,128)(2,1)}, bf16[1,1,16,128]{3,2,1,0:T(8,128)(2,1)}, f32[2,5,8,640]{3,2,1,0:T(8,128)}) custom-call(bf16[1,1,128,5120]{3,2,1,0:T(8,128)(2,1)} %conv_in.1, bf16[1,1,128,1024]{3,2,1,0:T(8,128)(2,1)} %gate_in.1, ...), custom_call_target="tpu_custom_call" | custom-call | tf_op jit(solution)/shard_map/mixer_tick/pallas_call | solution.py:733
  49.9 3.1 %mixer_finish.1 = (bf16[1,1,128,1024]{3,2,1,0:T(8,128)(2,1)}, bf16[1,1,128,5120]{3,2,1,0:T(8,128)(2,1)}, bf16[1,1,128,1024]{3,2,1,0:T(8,128)(2,1)}, bf16[1,1,16,...) custom-call(bf16[1,1,128,1024]{3,2,1,0:T(8,128)(2,1)} %get-tuple-ele, ...), custom_call_target="tpu_custom_call" | custom-call | tf_op jit(solution)/shard_map/mixer_finish/pallas_call | solution.py:751
